TPU v7x, 32 devices: a whole 2x2x4 slice. The times are simulated.
32 devices in a mesh: row: 8 (over y, x, core), col: 4 (over z).
Axes of the slice: x: 2, y: 2, z: 4, core: 2. Of those that a mesh axis runs over, the one named last changes fastest.
Arguments:
- points: bfloat16 [16, 16384], P(None, ('row', 'col')), may hold values from -6 to 6
- spread: bfloat16 [16384], P(('row', 'col')), may hold values from 2 to 12
- vectors: bfloat16 [8, 16384], P(None, ('row', 'col')), may hold values from -6 to 6
Outputs:
- basis: float32 [8, 16384], P(None, ('row', 'col'))
All inputs are finite; a program needn't handle non-finite values.
Results may differ from a plain program's by a relative error of at most 0.012.
Values may be sent and summed in bfloat16 or wider, within the bound.
No kernel may reach another device: no remote copies, remote signals or barrier semaphores. Data moves between devices by JAX's collectives and lax.ppermute only.
A program may use at most 64 MiB of HBM per device.

v0:
```python
import math
import jax
import jax.numpy as jnp
from jax import lax
from jax.sharding import PartitionSpec as P


def squared_norm(pts):
    values = pts.astype(jnp.float32)
    return jnp.sum(values * values, axis=0)


def affinity_block(pts_left, norm_left, scale_left, pts_right, norm_right, scale_right):
    cross = lax.dot_general(
        pts_left, pts_right, (((0,), (0,)), ((), ())), preferred_element_type=jnp.float32
    )
    dist = norm_left[:, None] + norm_right[None, :] - 2.0 * cross
    denom = scale_left.astype(jnp.float32)[:, None] * scale_right.astype(jnp.float32)[None, :]
    return jnp.exp(-dist / denom).astype(jnp.bfloat16)


def with_ones(vecs):
    return jnp.concatenate([vecs, jnp.ones((1,) + vecs.shape[1:], jnp.bfloat16)], axis=0)


def shards(points, spread, vectors):
    n_row = lax.axis_size("row")
    n_col = lax.axis_size("col")
    local = points.shape[1]
    dims = points.shape[0]
    kvec = vectors.shape[0]
    col_pts, col_scale, col_vecs = (
        lax.all_gather(points, "row", axis=1, tiled=True),
        lax.all_gather(spread, "row", axis=0, tiled=True),
        lax.all_gather(vectors, "row", axis=1, tiled=True),
    )
    col_ext = with_ones(col_vecs)
    col_norm = squared_norm(col_pts)
    row_pts, row_scale = (
        lax.all_gather(points, "col", axis=1, tiled=True),
        lax.all_gather(spread, "col", axis=0, tiled=True),
    )
    row_norm = squared_norm(row_pts)
    group = math.gcd(n_col, max(1, 512 // local))
    size = group * local
    nblocks = n_col // group
    pts_blocks = jnp.transpose(row_pts.reshape(dims, nblocks, size), (1, 0, 2))
    norm_blocks = row_norm.reshape(nblocks, size)
    scale_blocks = row_scale.reshape(nblocks, size)

    def one_block(operands):
        pts_blk, norm_blk, scale_blk = operands
        affinity = affinity_block(pts_blk, norm_blk, scale_blk, col_pts, col_norm, col_scale)
        return lax.dot_general(
            col_ext, affinity, (((1,), (1,)), ((), ())), preferred_element_type=jnp.float32
        )

    parts = lax.map(one_block, (pts_blocks, norm_blocks, scale_blocks))
    row_part = jnp.transpose(parts, (1, 0, 2)).reshape(kvec + 1, n_col * local)
    total = lax.psum_scatter(row_part, "col", scatter_dimension=1, tiled=True)
    update = total[:kvec] / total[kvec : kvec + 1]
    gram_local = jnp.sum(update[:, None, :] * update[None, :, :], axis=2)
    gram = lax.psum(gram_local, ("row", "col"))
    lower = jnp.linalg.cholesky(gram)
    solved = lax.linalg.triangular_solve(lower, update, left_side=True, lower=True)
    count = local * n_row * n_col
    return jnp.sqrt(jnp.float32(count)) * solved


def solution(mesh):
    in_specs = (P(None, ("row", "col")), P(("row", "col")), P(None, ("row", "col")))
    out_specs = P(None, ("row", "col"))
    return jax.shard_map(shards, mesh=mesh, in_specs=in_specs, out_specs=out_specs, check_vma=False)
```

profile of v0, /device:TPU:10, one launch (start us, length us, event | category | flops | bytes accessed | tf_op | source)
XLA Modules:
  0.0 145.8 jit_solution(7254464226759847502)
XLA Ops:
  6.5 0.0 reduce-scatter.2.cloned.1.call-start
  6.5 13.7 %all_gather.15 = bf16[16,2048]{1,0:T(8,128)(2,1)S(1)} all-gather(bf16[16,512]{1,0:T(8,128)(2,1)} %param.5), channel_id=1, replica_groups=mesh['row'=8,'col'=4] {'col'}, dimensions={1}, use_global_device_ids=true | all-gather | bytes 81920 | tf_op jit(solution)/shard_map/all_gather | solution.py:40
  20.3 9.2 %all_gather.16 = bf16[16,4096]{1,0:T(8,128)(2,1)S(1)} all-gather(bf16[16,512]{1,0:T(8,128)(2,1)} %param.5), channel_id=1, replica_groups=mesh['row'=8,'col'=4] {'row'}, dimensions={1}, use_global_device_ids=true | all-gather | bytes 147456 | tf_op jit(solution)/shard_map/all_gather | solution.py:33
  29.5 0.0 copy-start.1
  29.6 0.6 copy-done.1
  30.2 8.1 %all-gather.1 = bf16[8,1,512]{2,1,0:T(2,128)(2,1)S(1)} all-gather(bf16[1,1,512]{2,1,0:T(2,128)(2,1)S(1)} %reshape.41), channel_id=1, replica_groups=mesh['row'=8,'col'=4] {'row'}, dimensions={0}, use_global_device_ids=true | all-gather | bytes 9216 | tf_op jit(solution)/shard_map/all_gather | solution.py:34
  38.3 11.9 %all-gather = bf16[4,1,512]{2,1,0:T(2,128)(2,1)S(1)} all-gather(bf16[1,1,512]{2,1,0:T(2,128)(2,1)S(1)} %reshape.41), channel_id=1, replica_groups=mesh['row'=8,'col'=4] {'col'}, dimensions={0}, use_global_device_ids=true | all-gather | bytes 5120 | tf_op jit(solution)/shard_map/all_gather | solution.py:41
  50.2 0.0 copy-start
  50.3 0.1 multiply_reduce_fusion
  50.3 0.1 reduce.6
  50.4 0.5 copy-done
  50.9 9.0 %all_gather.19 = bf16[8,4096]{1,0:T(8,128)(2,1)S(1)} all-gather(bf16[8,512]{1,0:T(8,128)(2,1)S(1)} %copy-done), channel_id=1, replica_groups=mesh['row'=8,'col'=4] {'row'}, dimensions={1}, use_global_device_ids=true | all-gather | bytes 73728 | tf_op jit(solution)/shard_map/all_gather | solution.py:35
  60.0 14.6 %while.10 = (s32[]{:T(128)}, f32[4,9,512]{2,1,0:T(8,128)S(1)}, f32[4,512]{1,0:T(4,128)S(1)}, f32[4096]{0:T(1024)S(1)}, bf16[4,16,512]{2,1,0:T(8,128)(2,1)S(1)}, ...) while((s32[]{:T(128)}, f32[4,9,512]{2,1,0:T(8,128)S(1)}, ...), condition=%wide.region_3.4_spmd, body=%wide.region_2.3_spmd.sunk | while | flops 119542272 | bytes 381037 | solution.py:58
  60.0 3.6 %fusion.23 = f32[4,9,512]{2,1,0:T(8,128)S(1)} fusion(f32[4,9,512]{2,1,0:T(8,128)S(1)} %get-tuple-element.173, s32[]{:T(128)} %get-tuple-element.172, bf16[9,4096]{1,0:T(8,128)(2,1)S(1)} %get-tuple-element.190, bf16[16,4096]{1,0:T(8,128)(2,1)S(1)} %get-tuple-element.187, f32[4096]{0:T(1024)S(1)} %convert_element_type.44, f32[512]{0:T(512)S(1)} %bitcast.53, ...), kind=kOutput, calls=%fused_computation.3.clone.1 | convolution fusion | flops 119537664 | bytes 349184 | tf_op jit(solution)/shard_map/while/body/eval_jaxpr/dot_general | solution.py:54
  63.7 3.6 %fusion.23 = f32[4,9,512]{2,1,0:T(8,128)S(1)} fusion(f32[4,9,512]{2,1,0:T(8,128)S(1)} %get-tuple-element.173, s32[]{:T(128)} %get-tuple-element.172, bf16[9,4096]{1,0:T(8,128)(2,1)S(1)} %get-tuple-element.190, bf16[16,4096]{1,0:T(8,128)(2,1)S(1)} %get-tuple-element.187, f32[4096]{0:T(1024)S(1)} %convert_element_type.44, f32[512]{0:T(512)S(1)} %bitcast.53, ...), kind=kOutput, calls=%fused_computation.3.clone.1 | convolution fusion | flops 119537664 | bytes 349184 | tf_op jit(solution)/shard_map/while/body/eval_jaxpr/dot_general | solution.py:54
  67.3 3.6 %fusion.23 = f32[4,9,512]{2,1,0:T(8,128)S(1)} fusion(f32[4,9,512]{2,1,0:T(8,128)S(1)} %get-tuple-element.173, s32[]{:T(128)} %get-tuple-element.172, bf16[9,4096]{1,0:T(8,128)(2,1)S(1)} %get-tuple-element.190, bf16[16,4096]{1,0:T(8,128)(2,1)S(1)} %get-tuple-element.187, f32[4096]{0:T(1024)S(1)} %convert_element_type.44, f32[512]{0:T(512)S(1)} %bitcast.53, ...), kind=kOutput, calls=%fused_computation.3.clone.1 | convolution fusion | flops 119537664 | bytes 349184 | tf_op jit(solution)/shard_map/while/body/eval_jaxpr/dot_general | solution.py:54
  71.0 3.6 %fusion.23 = f32[4,9,512]{2,1,0:T(8,128)S(1)} fusion(f32[4,9,512]{2,1,0:T(8,128)S(1)} %get-tuple-element.173, s32[]{:T(128)} %get-tuple-element.172, bf16[9,4096]{1,0:T(8,128)(2,1)S(1)} %get-tuple-element.190, bf16[16,4096]{1,0:T(8,128)(2,1)S(1)} %get-tuple-element.187, f32[4096]{0:T(1024)S(1)} %convert_element_type.44, f32[512]{0:T(512)S(1)} %bitcast.53, ...), kind=kOutput, calls=%fused_computation.3.clone.1 | convolution fusion | flops 119537664 | bytes 349184 | tf_op jit(solution)/shard_map/while/body/eval_jaxpr/dot_general | solution.py:54
  74.6 0.1 copy.19
  74.7 0.7 copy.25
  75.4 0.0 reduce-scatter.2.cloned.1.call-update
  75.4 15.6 %reduce-scatter.2.cloned.1.call-done = f32[9,512]{1,0:T(8,128)} async-done(((f32[9,2048]{1,0:T(8,128)}), f32[9,512]{1,0:T(8,128)}) %reduce-scatter.2.cloned.1.call-update) | async-done | bytes 18448 | tf_op jit(solution)/shard_map/reduce_scatter | solution.py:60
  91.0 0.7 slice.19
  91.7 0.7 slice_divide_fusion
  92.4 0.1 multiply_reduce_fusion.1
  92.5 0.1 copy.20
  92.6 42.8 %psum.7 = f32[8,8]{0,1:T(8,128)S(1)} all-reduce(f32[8,8]{0,1:T(8,128)S(1)} %copy.20), channel_id=1, replica_groups=mesh['row'=8,'col'=4] {'row','col'}, use_global_device_ids=true, to_apply=%region_6.7 | all-reduce | flops 64 | bytes 512 | tf_op jit(solution)/shard_map/psum | solution.py:63
  135.4 0.1 copy.21
  135.5 0.7 cholesky.16
  136.2 0.6 compare_reduce_fusion
  136.9 0.6 fusion.10
  137.5 0.6 custom-call.6
  138.1 0.8 convolution_multiply_fusion
  (24 shorter events, 0.3 us)
Async XLA Ops:
  6.5 84.5 %reduce-scatter.2.cloned.1.call-start = ((), (), s32[]{:S(2)}) async-start(), calls=%async_computation.1 | async-start | bytes 163840 | tf_op jit(solution)/shard_map/reduce_scatter | solution.py:60
  29.5 0.7 copy-start.1
  50.2 0.7 copy-start
Sparse Core Ops, SparseCore 0:
  75.5 15.4 reduce-scatter.1
where the time goes:
time: 147 us; the launch traced here: 146 us
  blocking collectives  94.8 us (64%)
  waiting for transfers between devices  15.6 us (11%)
  matrix products  15.2 us (10%)
  between operations  13.5 us (9%)
  other arithmetic  3.67 us (2%)
  local copies, waits for them, and re-layouts  2.89 us (2%)
    psum x1, blocking collectives, shards(): gram = lax.psum(gram_local, ('row', 'col'))  42.8 us
    reduce_scatter x1, waiting for transfers between devices, shards(): total = lax.psum_scatter(row_part, 'col', scatter_dimension=1, tiled=True)  15.6 us
    dot_general x4, matrix products, one_block(): lax.dot_general(col_ext, affinity, (((1,), (1,)), ((), ())), preferred_el...  14.4 us
    all_gather x1, blocking collectives, shards(): lax.all_gather(points, 'col', axis=1, tiled=True)  13.7 us
    all_gather x1, blocking collectives, shards(): lax.all_gather(spread, 'col', axis=0, tiled=True)  11.9 us
    all_gather x1, blocking collectives, shards(): lax.all_gather(points, 'row', axis=1, tiled=True)  9.23 us
    all_gather x1, blocking collectives, shards(): lax.all_gather(vectors, 'row', axis=1, tiled=True)  9.03 us
    all_gather x1, blocking collectives, shards(): lax.all_gather(spread, 'row', axis=0, tiled=True)  8.1 us
  transfers between devices with their start and end apart: 1, of which 1 were waited for; matrix products, arithmetic and copies ran while one was open for 0% of the time, Pallas kernels for 0%

commit v1 on v0

--- a/solution.py
+++ b/solution.py
@@ -3,6 +3,11 @@
 import jax.numpy as jnp
 from jax import lax
 from jax.sharding import PartitionSpec as P
+
+
+def widths_solve(across, mat):
+    y_new = lax.all_gather(mat, across)
+    return jnp.sum(y_new, axis=0)
 
 
 def squared_norm(pts):
@@ -60,7 +65,7 @@
     total = lax.psum_scatter(row_part, "col", scatter_dimension=1, tiled=True)
     update = total[:kvec] / total[kvec : kvec + 1]
     gram_local = jnp.sum(update[:, None, :] * update[None, :, :], axis=2)
-    gram = lax.psum(gram_local, ("row", "col"))
+    gram = widths_solve(("row", "col"), gram_local)
     lower = jnp.linalg.cholesky(gram)
     solved = lax.linalg.triangular_solve(lower, update, left_side=True, lower=True)
     count = local * n_row * n_col

time: 147 us -> 172 us (1.17)
  the two profiles are of different devices: /device:TPU:10 before, /device:TPU:0 now
where the time goes in v1:
time: 172 us
  blocking collectives  118 us (69%)
  waiting for transfers between devices  18.5 us (11%)
  matrix products  15.2 us (9%)
  between operations  13.5 us (8%)
  other arithmetic  3.7 us (2%)
  local copies, waits for them, and re-layouts  2.82 us (2%)
    all_gather x1, blocking collectives, widths_solve(): y_new = lax.all_gather(mat, across)  64.3 us
    reduce_scatter x1, waiting for transfers between devices, shards(): total = lax.psum_scatter(row_part, 'col', scatter_dimension=1, tiled=True)  18.5 us
    all_gather x1, blocking collectives, shards(): lax.all_gather(points, 'col', axis=1, tiled=True)  15.1 us
    dot_general x4, matrix products, one_block(): lax.dot_general(col_ext, affinity, (((1,), (1,)), ((), ())), preferred_el...  14.4 us
    all_gather x1, blocking collectives, shards(): lax.all_gather(spread, 'col', axis=0, tiled=True)  11.9 us
    all_gather x1, blocking collectives, shards(): lax.all_gather(points, 'row', axis=1, tiled=True)  9.41 us
    all_gather x1, blocking collectives, shards(): lax.all_gather(spread, 'row', axis=0, tiled=True)  8.71 us
    all_gather x1, blocking collectives, shards(): lax.all_gather(vectors, 'row', axis=1, tiled=True)  8.43 us
  transfers between devices with their start and end apart: 1, of which 1 were waited for; matrix products, arithmetic and copies ran while one was open for 0% of the time, Pallas kernels for 0%

profile of v1, /device:TPU:0, one launch (start us, length us, event | category | flops | bytes accessed | tf_op | source)
XLA Modules:
  0.0 171.7 jit_solution(206027055505077796)
XLA Ops:
  6.5 0.0 reduce-scatter.2.cloned.1.call-start
  6.5 15.1 %all_gather.21 = bf16[16,2048]{1,0:T(8,128)(2,1)S(1)} all-gather(bf16[16,512]{1,0:T(8,128)(2,1)} %param.5), channel_id=1, replica_groups=mesh['row'=8,'col'=4] {'col'}, dimensions={1}, use_global_device_ids=true | all-gather | bytes 81920 | tf_op jit(solution)/shard_map/all_gather | solution.py:45
  21.7 9.4 %all_gather.22 = bf16[16,4096]{1,0:T(8,128)(2,1)S(1)} all-gather(bf16[16,512]{1,0:T(8,128)(2,1)} %param.5), channel_id=1, replica_groups=mesh['row'=8,'col'=4] {'row'}, dimensions={1}, use_global_device_ids=true | all-gather | bytes 147456 | tf_op jit(solution)/shard_map/all_gather | solution.py:38
  31.1 0.0 copy-start.1
  31.1 0.6 copy-done.1
  31.8 8.7 %all-gather.2 = bf16[8,1,512]{2,1,0:T(2,128)(2,1)S(1)} all-gather(bf16[1,1,512]{2,1,0:T(2,128)(2,1)S(1)} %reshape.42), channel_id=1, replica_groups=mesh['row'=8,'col'=4] {'row'}, dimensions={0}, use_global_device_ids=true | all-gather | bytes 9216 | tf_op jit(solution)/shard_map/all_gather | solution.py:39
  40.5 11.9 %all-gather.1 = bf16[4,1,512]{2,1,0:T(2,128)(2,1)S(1)} all-gather(bf16[1,1,512]{2,1,0:T(2,128)(2,1)S(1)} %reshape.42), channel_id=1, replica_groups=mesh['row'=8,'col'=4] {'col'}, dimensions={0}, use_global_device_ids=true | all-gather | bytes 5120 | tf_op jit(solution)/shard_map/all_gather | solution.py:46
  52.4 0.0 copy-start
  52.4 0.1 multiply_reduce_fusion
  52.5 0.1 reduce.6
  52.6 0.5 copy-done
  53.1 8.4 %all_gather.25 = bf16[8,4096]{1,0:T(8,128)(2,1)S(1)} all-gather(bf16[8,512]{1,0:T(8,128)(2,1)S(1)} %copy-done), channel_id=1, replica_groups=mesh['row'=8,'col'=4] {'row'}, dimensions={1}, use_global_device_ids=true | all-gather | bytes 73728 | tf_op jit(solution)/shard_map/all_gather | solution.py:40
  61.6 14.6 %while.10 = (s32[]{:T(128)}, f32[4,9,512]{2,1,0:T(8,128)S(1)}, f32[4,512]{1,0:T(4,128)S(1)}, f32[4096]{0:T(1024)S(1)}, bf16[4,16,512]{2,1,0:T(8,128)(2,1)S(1)}, ...) while((s32[]{:T(128)}, f32[4,9,512]{2,1,0:T(8,128)S(1)}, ...), condition=%wide.region_3.4_spmd, body=%wide.region_2.3_spmd.sunk | while | flops 119542272 | bytes 381037 | solution.py:63
  61.6 3.6 %fusion.23 = f32[4,9,512]{2,1,0:T(8,128)S(1)} fusion(f32[4,9,512]{2,1,0:T(8,128)S(1)} %get-tuple-element.173, s32[]{:T(128)} %get-tuple-element.172, bf16[9,4096]{1,0:T(8,128)(2,1)S(1)} %get-tuple-element.190, bf16[16,4096]{1,0:T(8,128)(2,1)S(1)} %get-tuple-element.187, f32[4096]{0:T(1024)S(1)} %convert_element_type.44, f32[512]{0:T(512)S(1)} %bitcast.55, ...), kind=kOutput, calls=%fused_computation.3.clone.1 | convolution fusion | flops 119537664 | bytes 349184 | tf_op jit(solution)/shard_map/while/body/eval_jaxpr/dot_general | solution.py:59
  65.3 3.6 %fusion.23 = f32[4,9,512]{2,1,0:T(8,128)S(1)} fusion(f32[4,9,512]{2,1,0:T(8,128)S(1)} %get-tuple-element.173, s32[]{:T(128)} %get-tuple-element.172, bf16[9,4096]{1,0:T(8,128)(2,1)S(1)} %get-tuple-element.190, bf16[16,4096]{1,0:T(8,128)(2,1)S(1)} %get-tuple-element.187, f32[4096]{0:T(1024)S(1)} %convert_element_type.44, f32[512]{0:T(512)S(1)} %bitcast.55, ...), kind=kOutput, calls=%fused_computation.3.clone.1 | convolution fusion | flops 119537664 | bytes 349184 | tf_op jit(solution)/shard_map/while/body/eval_jaxpr/dot_general | solution.py:59
  68.9 3.6 %fusion.23 = f32[4,9,512]{2,1,0:T(8,128)S(1)} fusion(f32[4,9,512]{2,1,0:T(8,128)S(1)} %get-tuple-element.173, s32[]{:T(128)} %get-tuple-element.172, bf16[9,4096]{1,0:T(8,128)(2,1)S(1)} %get-tuple-element.190, bf16[16,4096]{1,0:T(8,128)(2,1)S(1)} %get-tuple-element.187, f32[4096]{0:T(1024)S(1)} %convert_element_type.44, f32[512]{0:T(512)S(1)} %bitcast.55, ...), kind=kOutput, calls=%fused_computation.3.clone.1 | convolution fusion | flops 119537664 | bytes 349184 | tf_op jit(solution)/shard_map/while/body/eval_jaxpr/dot_general | solution.py:59
  72.5 3.6 %fusion.23 = f32[4,9,512]{2,1,0:T(8,128)S(1)} fusion(f32[4,9,512]{2,1,0:T(8,128)S(1)} %get-tuple-element.173, s32[]{:T(128)} %get-tuple-element.172, bf16[9,4096]{1,0:T(8,128)(2,1)S(1)} %get-tuple-element.190, bf16[16,4096]{1,0:T(8,128)(2,1)S(1)} %get-tuple-element.187, f32[4096]{0:T(1024)S(1)} %convert_element_type.44, f32[512]{0:T(512)S(1)} %bitcast.55, ...), kind=kOutput, calls=%fused_computation.3.clone.1 | convolution fusion | flops 119537664 | bytes 349184 | tf_op jit(solution)/shard_map/while/body/eval_jaxpr/dot_general | solution.py:59
  76.1 0.1 copy.19
  76.2 0.7 copy.26
  76.9 0.0 reduce-scatter.2.cloned.1.call-update
  77.0 18.5 %reduce-scatter.2.cloned.1.call-done = f32[9,512]{1,0:T(8,128)} async-done(((f32[9,2048]{1,0:T(8,128)}), f32[9,512]{1,0:T(8,128)}) %reduce-scatter.2.cloned.1.call-update) | async-done | bytes 18448 | tf_op jit(solution)/shard_map/reduce_scatter | solution.py:65
  95.4 0.7 slice.19
  96.1 0.7 slice_divide_fusion
  96.8 0.1 multiply_reduce_fusion.1
  96.9 64.3 %all-gather = f32[256,8]{1,0:T(8,128)S(1)} all-gather(f32[8,8]{1,0:T(8,128)S(1)} %multiply_reduce_fusion.1), channel_id=2, replica_groups=mesh['row'=8,'col'=4] {'row','col'}, dimensions={0}, use_global_device_ids=true | all-gather | bytes 8448 | tf_op jit(solution)/shard_map/all_gather | solution.py:9
  161.3 0.1 copy.21
  161.4 0.7 cholesky.16
  162.1 0.6 compare_reduce_fusion
  162.8 0.6 fusion.10
  163.5 0.6 custom-call.6
  164.1 0.8 convolution_multiply_fusion
  (25 shorter events, 0.3 us)
Async XLA Ops:
  6.5 88.9 %reduce-scatter.2.cloned.1.call-start = ((), (), s32[]{:S(2)}) async-start(), calls=%async_computation.1 | async-start | bytes 163840 | tf_op jit(solution)/shard_map/reduce_scatter | solution.py:65
  31.1 0.7 copy-start.1
  52.4 0.7 copy-start
Sparse Core Ops, SparseCore 0:
  77.1 18.2 reduce-scatter.1
